TPU v7x, 32 devices: a whole 2x2x4 slice. The times are simulated.
32 devices in a mesh: dev: 8 (over z, y), rep: 4 (over x, core).
Axes of the slice: x: 2, y: 2, z: 4, core: 2. Of those that a mesh axis runs over, the one named last changes fastest.
Arguments:
- spins: int32 [8, 64], P('dev'), may hold values 0 or 1
- activations: float32 [4, 8, 64, 128], P('rep', 'dev'), may hold values from 0 to 0.5
- gradients: float32 [4, 8, 64, 256], P('rep', 'dev'), may hold values from -0.1 to 0.3
Outputs:
- gram: float32 [8, 8], P('dev', 'rep')
Inputs may be any that keep to these rules, and one draw needn't show every extreme that they name: `spins`: 1 marks an occupied site, 0 an empty one.
All inputs are finite; a program needn't handle non-finite values. No bound on the sum of `spins` on one device may be relied on, other than what follows from the above.
Results may differ from a plain program's by a relative error of at most 0.0001.
Values sent between devices are 32-bit elements; how exact they have to be, the bound alone decides.
No kernel may reach another device: no remote copies, remote signals or barrier semaphores. Data moves between devices by JAX's collectives and lax.ppermute only.
A program may use at most 128 MiB of HBM per device.

v0:
```python
import jax
import jax.numpy as jnp
from jax import lax
from jax.sharding import PartitionSpec as P


def form_scores(act, grad, occupied):
    weighted = act * occupied[None, :, :, None]
    score = jnp.einsum("psra,psrb->spab", weighted, grad, precision=lax.Precision.HIGHEST)
    return score.reshape(score.shape[0], score.shape[1], -1)


def body(spins, activations, gradients):
    occupied = spins.astype(jnp.float32)
    all_act, all_grad = (
        lax.all_gather(activations, "rep", axis=0, tiled=True),
        lax.all_gather(gradients, "rep", axis=0, tiled=True),
    )
    score = form_scores(all_act, all_grad, occupied)
    moved = lax.all_to_all(score, "dev", split_axis=2, concat_axis=0, tiled=True)
    total = moved.shape[0]
    centered = moved - jnp.mean(moved, axis=0, keepdims=True)
    width = total // lax.axis_size("rep")
    begin = lax.axis_index("rep") * width
    columns = lax.dynamic_slice_in_dim(centered, begin, width, 0)
    partial_gram = jnp.einsum("spa,tpa->st", centered, columns, precision=lax.Precision.HIGHEST)
    return lax.psum_scatter(partial_gram / total, "dev", scatter_dimension=0, tiled=True)


def solution(mesh):
    return jax.shard_map(
        body,
        mesh=mesh,
        in_specs=(P("dev", None), P("rep", "dev", None, None), P("rep", "dev", None, None)),
        out_specs=P("dev", "rep"),
        check_vma=False,
    )
```

profile of v0, /device:TPU:0, one launch (start us, length us, event | category | flops | bytes accessed | tf_op | source)
XLA Modules:
  0.0 278.7 jit_solution(6322244386527385481)
XLA Ops:
  0.0 7.4 %all_gather.7 = f32[4,1,64,256]{3,2,1,0:T(8,128)S(1)} all-gather(f32[1,1,64,256]{3,2,1,0:T(8,128)} %param.5), channel_id=1, replica_groups=mesh['dev'=8,'rep'=4] {'rep'}, dimensions={0}, use_global_device_ids=true | all-gather | bytes 327680 | tf_op jit(solution)/shard_map/all_gather | solution.py:17
  7.4 5.6 %all_gather.6 = f32[4,1,64,128]{3,2,1,0:T(8,128)S(1)} all-gather(f32[1,1,64,128]{3,2,1,0:T(8,128)} %param.4), channel_id=1, replica_groups=mesh['dev'=8,'rep'=4] {'rep'}, dimensions={0}, use_global_device_ids=true | all-gather | bytes 163840 | tf_op jit(solution)/shard_map/all_gather | solution.py:16
  13.0 0.7 convert_bitcast_fusion
  13.7 0.7 fusion.1
  14.4 8.7 %copy.7 = f32[4,128,256]{0,2,1:T(8,128)} copy(f32[4,128,256]{2,1,0:T(8,128)S(1)} %fusion.1) | data formatting | bytes 1048576 | tf_op jit(solution)/shard_map/reshape | solution.py:10
  23.1 0.5 broadcast.13
  23.6 146.5 %reduce.1 = f32[32768,4]{1,0:T(8,128)} reduce(f32[32768,1,4]{2,1,0:T(1,128)} %bitcast.23, f32[]{:T(128)} %broadcast.13), dimensions={1}, to_apply=%bitcast.20.reduce_sub_computation | reduce | bytes 1048580
  170.1 16.0 %reshape.23 = f32[8,1,16384]{2,1,0:T(1,128)} reshape(f32[32768,4]{1,0:T(8,128)} %reduce.1) | data formatting | bytes 1048576
  186.1 5.9 %all-to-all-start = ((f32[8,1,16384]{2,1,0:T(1,128)}), f32[8,1,16384]{2,1,0:T(1,128)S(1)}, u32[]{:S(2)}, u32[]{:S(2)}) async-start(f32[8,1,16384]{2,1,0:T(1,128)} %reshape.23), calls=%async_computation | async-start | bytes 1048576 | tf_op jit(solution)/shard_map/all_to_all | solution.py:20
  191.9 15.0 %all-to-all-done = f32[8,1,16384]{2,1,0:T(1,128)S(1)} async-done(((f32[8,1,16384]{2,1,0:T(1,128)}), f32[8,1,16384]{2,1,0:T(1,128)S(1)}, u32[]{:S(2)}, u32[]{:S(2)}) %all-to-all-start) | async-done | bytes 524320 | tf_op jit(solution)/shard_map/all_to_all | solution.py:20
  206.9 1.9 reduce.2
  208.8 0.0 copy-start
  208.8 37.3 %reshape.24 = f32[32768,1,4]{2,1,0:T(1,128)} reshape(f32[8,16384]{1,0:T(8,128)S(1)} %reduce.2) | data formatting | bytes 1048576
  246.1 9.8 %copy.8 = f32[1,4,8,4096]{3,2,1,0:T(8,128)S(1)} copy(f32[1,4,8,4096]{1,3,2,0:T(8,128)} %bitcast.24) | data formatting | bytes 1048576 | tf_op jit(solution)/shard_map/all_to_all | solution.py:20
  255.9 0.1 bitcast_reduce_fusion
  256.1 0.1 bitcast_subtract_fusion
  256.1 1.2 fusion
  257.3 0.0 copy-done
  257.3 0.7 dynamic-slice
  258.0 19.5 %all-reduce = f32[8,2]{1,0:T(8,128)S(1)} all-reduce(f32[8,2]{1,0:T(8,128)S(1)} %fusion), channel_id=2, replica_groups=mesh['dev'=8,'rep'=4] {'dev'}, use_global_device_ids=true, to_apply=%region_1.0.clone | all-reduce | flops 16 | bytes 128
  277.5 1.2 constant_dynamic-slice_fusion
  (1 shorter events, 0.0 us)
Async XLA Ops:
  186.1 20.9 %all-to-all-start = ((f32[8,1,16384]{2,1,0:T(1,128)}), f32[8,1,16384]{2,1,0:T(1,128)S(1)}, u32[]{:S(2)}, u32[]{:S(2)}) async-start(f32[8,1,16384]{2,1,0:T(1,128)} %reshape.23), calls=%async_computation | async-start | bytes 1048576 | tf_op jit(solution)/shard_map/all_to_all | solution.py:20
  208.8 48.5 %copy-start = (u32[32]{0:T(128)S(1)}, u32[32]{0:T(128)}, u32[]{:S(2)}) copy-start(u32[32]{0:T(128)} %constant.22) | copy-start | bytes 388
where the time goes:
time: 279 us
  other arithmetic  149 us (53%)
  local copies, waits for them, and re-layouts  74.1 us (27%)
  blocking collectives  32.5 us (12%)
  waiting for transfers between devices  15 us (5%)
  starting transfers between devices  5.88 us (2%)
    unnamed x1, other arithmetic  147 us
    unnamed x7, local copies, waits for them, and re-layouts  55.7 us
    unnamed x1, blocking collectives  19.5 us
    all_to_all x1, waiting for transfers between devices, body(): lax.all_to_all(score, 'dev', split_axis=2, concat_axis=0, tiled=True)  15 us
    all_to_all x1, local copies, waits for them, and re-layouts, body(): lax.all_to_all(score, 'dev', split_axis=2, concat_axis=0, tiled=True)  9.77 us
    reshape x1, local copies, waits for them, and re-layouts, form_scores(): return score.reshape(score.shape[0], score.shape[1], -1)  8.65 us
    all_gather x1, blocking collectives, body(): lax.all_gather(gradients, 'rep', axis=0, tiled=True)  7.42 us
    all_to_all x1, starting transfers between devices, body(): lax.all_to_all(score, 'dev', split_axis=2, concat_axis=0, tiled=True)  5.88 us
  transfers between devices with their start and end apart: 1, of which 1 were waited for; matrix products, arithmetic and copies ran while one was open for 0% of the time, Pallas kernels for 0%

commit v1 on v0

--- a/solution.py
+++ b/solution.py
@@ -17,7 +17,10 @@
         lax.all_gather(gradients, "rep", axis=0, tiled=True),
     )
     score = form_scores(all_act, all_grad, occupied)
-    moved = lax.all_to_all(score, "dev", split_axis=2, concat_axis=0, tiled=True)
+    moved = jnp.concatenate(
+        lax.all_to_all(jnp.stack(jnp.split(score, lax.axis_size("dev"), axis=2)), "dev", 0, 0),
+        axis=0,
+    )
     total = moved.shape[0]
     centered = moved - jnp.mean(moved, axis=0, keepdims=True)
     width = total // lax.axis_size("rep")

time: 279 us -> 63.3 us (0.23)
  other arithmetic: 149 us -> 0.42 us
  local copies, waits for them, and re-layouts: 74.1 us -> 7.15 us
    unnamed x1 -> x0, other arithmetic: 147 us -> none
    unnamed x7 -> x15, local copies, waits for them, and re-layouts: 55.7 us -> 6.27 us
    all_to_all x1 -> x0, local copies, waits for them, and re-layouts: 9.77 us -> none  [body(): lax.all_to_all(score, 'dev', split_axis=2, concat_axis=0, tiled=True)]
    reshape x1, local copies, waits for them, and re-layouts: 8.65 us -> 0.26 us  [form_scores(): return score.reshape(score.shape[0], score.shape[1], -1)]
where the time goes in v1:
time: 63.3 us; the launch traced here: 63 us
  blocking collectives  32.5 us (51%)
  waiting for transfers between devices  15 us (24%)
  local copies, waits for them, and re-layouts  7.15 us (11%)
  starting transfers between devices  5.86 us (9%)
  matrix products  1.93 us (3%)
    unnamed x1, blocking collectives  19.5 us
    all_to_all x1, waiting for transfers between devices, body(): lax.all_to_all(jnp.stack(jnp.split(score, lax.axis_size('dev'), axis=2)),...  15 us
    all_gather x1, blocking collectives, body(): lax.all_gather(gradients, 'rep', axis=0, tiled=True)  7.55 us
    unnamed x15, local copies, waits for them, and re-layouts  6.27 us
    all_to_all x1, starting transfers between devices, body(): lax.all_to_all(jnp.stack(jnp.split(score, lax.axis_size('dev'), axis=2)),...  5.86 us
    all_gather x1, blocking collectives, body(): lax.all_gather(activations, 'rep', axis=0, tiled=True)  5.53 us
  transfers between devices with their start and end apart: 1, of which 1 were waited for; matrix products, arithmetic and copies ran while one was open for 0% of the time, Pallas kernels for 0%

profile of v1, /device:TPU:0, one launch (start us, length us, event | category | flops | bytes accessed | tf_op | source)
XLA Modules:
  0.0 63.0 jit_solution(13747785996527098711)
XLA Ops:
  0.0 0.0 copy-start
  0.0 7.5 %all_gather.7 = f32[4,1,64,256]{3,2,1,0:T(8,128)S(1)} all-gather(f32[1,1,64,256]{3,2,1,0:T(8,128)} %param.5), channel_id=1, replica_groups=mesh['dev'=8,'rep'=4] {'rep'}, dimensions={0}, use_global_device_ids=true | all-gather | bytes 327680 | tf_op jit(solution)/shard_map/all_gather | solution.py:17
  7.6 0.0 copy-done
  7.6 0.0 copy-start.1
  7.6 5.5 %all_gather.6 = f32[4,1,64,128]{3,2,1,0:T(8,128)S(1)} all-gather(f32[1,1,64,128]{3,2,1,0:T(8,128)S(1)} %copy-done), channel_id=1, replica_groups=mesh['dev'=8,'rep'=4] {'rep'}, dimensions={0}, use_global_device_ids=true | all-gather | bytes 163840 | tf_op jit(solution)/shard_map/all_gather | solution.py:16
  13.1 0.0 copy-done.1
  13.1 0.7 %fusion.1 = f32[4,128,256]{2,1,0:T(8,128)S(1)} fusion(f32[4,1,64,256]{3,2,1,0:T(8,128)S(1)} %all_gather.7, f32[4,1,64,128]{3,2,1,0:T(8,128)S(1)} %all_gather.6, f32[64]{0:T(128)S(1)} %convert_bitcast_fusion), kind=kOutput, calls=%fused_computation.3 | convolution fusion | flops 100696064 | bytes 917760 | tf_op jit(solution)/shard_map/psra,psrb->spab/dot_general | solution.py:9
  13.8 0.3 reshape.23
  14.1 0.6 fusion.13
  14.7 0.6 fusion.12
  15.3 0.6 fusion.11
  15.9 0.6 fusion.10
  16.6 0.6 fusion.9
  17.2 0.6 %fusion.8 = f32[8,1,4,4096]{3,2,1,0:T(4,128)} fusion(f32[8,1,4,4096]{3,2,1,0:T(4,128)} %fusion.9, f32[1,4,32768]{2,1,0:T(4,128)S(1)} %reshape.23), kind=kLoop, calls=%fused_computation.13 | loop fusion | bytes 131072
  17.8 0.6 fusion.7
  18.4 0.6 fusion.6
  19.1 5.9 %all-to-all-start = ((f32[8,1,4,4096]{3,2,1,0:T(4,128)}), f32[8,1,4,4096]{3,2,1,0:T(4,128)S(1)}, u32[]{:S(2)}, u32[]{:S(2)}) async-start(f32[8,1,4,4096]{3,2,1,0:T(4,128)} %fusion.6), calls=%async_computation | async-start | bytes 1048576 | tf_op jit(solution)/shard_map/all_to_all | solution.py:21
  24.9 15.0 %all-to-all-done = f32[8,1,4,4096]{3,2,1,0:T(4,128)S(1)} async-done(((f32[8,1,4,4096]{3,2,1,0:T(4,128)}), f32[8,1,4,4096]{3,2,1,0:T(4,128)S(1)}, u32[]{:S(2)}, u32[]{:S(2)}) %all-to-all-start) | async-done | bytes 524320 | tf_op jit(solution)/shard_map/all_to_all | solution.py:21
  39.9 0.1 reduce_sum.9
  40.0 0.3 bitcast_subtract_fusion
  40.4 0.0 copy-start.2
  40.4 1.2 %fusion = f32[8,2]{1,0:T(8,128)S(1)} fusion(f32[8,4,4096]{2,0,1:T(8,128)S(1)} %bitcast_subtract_fusion, s32[]{:T(128)S(6)} %select_n.3), kind=kOutput, calls=%fused_computation.1 | convolution fusion | flops 3145744 | bytes 655428 | tf_op jit(solution)/shard_map/spa,tpa->st/dot_general | solution.py:29
  41.6 0.0 copy-done.2
  41.6 0.7 %dynamic-slice = u32[1]{0:T(128)} dynamic-slice(u32[32]{0:T(128)S(1)} %copy-done.2, u32[]{:T(128)S(6)} %add.7), dynamic_slice_sizes={1} | dynamic-slice | bytes 12
  42.3 19.5 %all-reduce = f32[8,2]{1,0:T(8,128)S(1)} all-reduce(f32[8,2]{1,0:T(8,128)S(1)} %fusion), channel_id=2, replica_groups=mesh['dev'=8,'rep'=4] {'dev'}, use_global_device_ids=true, to_apply=%region_1.0.clone | all-reduce | flops 16 | bytes 128
  61.8 1.2 %constant_dynamic-slice_fusion = f32[1,2]{1,0:T(1,128)} fusion(f32[8,2]{1,0:T(8,128)S(1)} %all-reduce, u32[]{:T(128)} %bitcast.13), kind=kLoop, calls=%fused_computation.26 | loop fusion | bytes 20
  (2 shorter events, 0.0 us)
Async XLA Ops:
  0.0 7.6 %copy-start = (f32[1,1,64,128]{3,2,1,0:T(8,128)S(1)}, f32[1,1,64,128]{3,2,1,0:T(8,128)}, u32[]{:S(2)}) copy-start(f32[1,1,64,128]{3,2,1,0:T(8,128)} %param.4) | copy-start | bytes 98308
  7.6 5.5 %copy-start.1 = (s32[1,64]{1,0:T(1,128)S(1)}, s32[1,64]{1,0:T(1,128)}, u32[]{:S(2)}) copy-start(s32[1,64]{1,0:T(1,128)} %param.3) | copy-start | bytes 772
  19.1 20.9 %all-to-all-start = ((f32[8,1,4,4096]{3,2,1,0:T(4,128)}), f32[8,1,4,4096]{3,2,1,0:T(4,128)S(1)}, u32[]{:S(2)}, u32[]{:S(2)}) async-start(f32[8,1,4,4096]{3,2,1,0:T(4,128)} %fusion.6), calls=%async_computation | async-start | bytes 1048576 | tf_op jit(solution)/shard_map/all_to_all | solution.py:21
  40.4 1.2 %copy-start.2 = (u32[32]{0:T(128)S(1)}, u32[32]{0:T(128)}, u32[]{:S(2)}) copy-start(u32[32]{0:T(128)} %constant.22) | copy-start | bytes 388
